TPU v7x, 512 devices: a whole 4x8x8 slice. The times are simulated.
512 devices in a mesh: chain: 2 (over x_lo), slab: 128 (over x_hi, z, y), vis: 2 (over core).
Axes of the slice: x: 4 (x_hi: 2, x_lo: 2; x = x_hi * 2 + x_lo), y: 8, z: 8, core: 2. Of those that a mesh axis runs over, the one named last changes fastest.
Arguments:
- screens: float32 [4, 2048, 2048], P(('chain', 'vis'), 'slab'), parts along dimension 0, may hold values from -6 to 6
- image: float32 [4096, 2048], P(('chain', 'slab')), parts along dimension 0, may hold values from -6 to 6
- vis_row: int32 [32768], P('slab'), may hold values from 0 to 2047
- vis_block: int32 [32768, 1], P('slab'), may hold values from 0 to 127; in each aligned block of 256 rows (0 to 255, 256 to 511, ...) at most 6 rows name the same one
- vis_column: int32 [32768], P('slab'), may hold values from 0 to 7
- vis_real: float32 [32768], P('slab'), may hold values from -6 to 6
- vis_imag: float32 [32768], P('slab'), may hold values from -6 to 6
- vis_weight: float32 [32768], P('slab'), may hold values from 0.5 to 4
Outputs:
- screen_grad: float32 [4, 2048, 2048], P(('chain', 'vis'), 'slab'), parts along dimension 0
There are 2 independent parts, one for each index of `chain`. A program takes and returns all parts, laid end to end along the dimension named above; an argument that names none is the same for every part. Nothing has to cross between parts.
Inputs may be any that keep to these rules, and one draw needn't show every extreme that they name: `vis_block`: among the 256 visibilities of one index of slab, at most 6 name any one block; in every draw some block of some index holds exactly 6.
All inputs are finite; a program needn't handle non-finite values.
Results may differ from a plain program's by a relative error of at most 0.013.
Values may be sent and summed in bfloat16 or wider, within the bound.
No kernel may reach another device: no remote copies, remote signals or barrier semaphores. Data moves between devices by JAX's collectives and lax.ppermute only.
A program may use at most 64 MiB of HBM per device.

v0:
```python
import math
import jax
import jax.numpy as jnp
from jax import lax
from jax.sharding import PartitionSpec as P

refract = 1.0
rank_rows = 512
sample_rows = 256
table_rows = 256


def with_halo(cells, sides, width):
    for axis, dim in sides:
        count = lax.axis_size(axis)
        head = lax.slice_in_dim(cells, 0, width, axis=dim)
        tail = lax.slice_in_dim(cells, cells.shape[dim] - width, cells.shape[dim], axis=dim)
        cells = jnp.concatenate(
            [
                lax.ppermute(tail, axis, [(i, (i + 1) % count) for i in range(count)]),
                cells,
                lax.ppermute(head, axis, [((i + 1) % count, i) for i in range(count)]),
            ],
            axis=dim,
        )
    return cells


def twiddle(first, second, length):
    phase = (first[:, None] * second[None, :] % length).astype(jnp.float32) * (
        2.0 * math.pi / length
    )
    return (jnp.cos(phase).astype(jnp.bfloat16), jnp.sin(phase).astype(jnp.bfloat16))


def col_slope(field):
    return (
        8.0 * (jnp.roll(field, -1, -1) - jnp.roll(field, 1, -1))
        - (jnp.roll(field, -2, -1) - jnp.roll(field, 2, -1))
    ) / 12.0


def col_adjoint(field):
    return (
        8.0 * (jnp.roll(field, 1, -1) - jnp.roll(field, -1, -1))
        - (jnp.roll(field, 2, -1) - jnp.roll(field, -2, -1))
    ) / 12.0


def row_slope(padded, row_count):
    return (
        8.0 * (padded[..., 3 : row_count + 3, :] - padded[..., 1 : row_count + 1, :])
        - (padded[..., 4 : row_count + 4, :] - padded[..., 0:row_count, :])
    ) / 12.0


def row_adjoint(padded, row_count):
    return (
        8.0 * (padded[..., 1 : row_count + 1, :] - padded[..., 3 : row_count + 3, :])
        - (padded[..., 0:row_count, :] - padded[..., 4 : row_count + 4, :])
    ) / 12.0


def local(screens, image, vis_row, vis_block, vis_column, vis_real, vis_imag, vis_weight):
    walkers, row_count, grid_size = screens.shape
    slabs = lax.axis_size("slab")
    half_kx = grid_size // 2
    vis_count = vis_row.shape[0]
    capacity = 3 * vis_count // slabs
    unitary = 1.0 / math.sqrt(grid_size)
    positions = jnp.arange(grid_size, dtype=jnp.int32)
    highest = lax.Precision.HIGHEST
    stacked = jnp.concatenate([screens, image[None]], axis=0)
    padded = with_halo(stacked.astype(jnp.bfloat16), (("slab", 1),), 2).astype(stacked.dtype)
    slope_x = col_slope(stacked)
    slope_y = row_slope(padded, row_count)
    joined = image[None] + refract * (
        slope_x[:walkers] * slope_x[walkers][None] + slope_y[:walkers] * slope_y[walkers][None]
    )
    joined_bf = joined.astype(jnp.bfloat16)
    owner_slab = vis_block[:, 0]
    owned = half_kx // slabs
    step_kx = min(table_rows, half_kx)
    real_parts = []
    imag_parts = []
    for offset in range(0, half_kx, step_kx):
        cos_rows, sin_rows = twiddle(
            offset + jnp.arange(step_kx, dtype=jnp.int32), positions, grid_size
        )
        with_cos = jnp.einsum(
            "kc,wrc->wkr", cos_rows, joined_bf, preferred_element_type=jnp.float32
        )
        with_sin = jnp.einsum(
            "kc,wrc->wkr", sin_rows, joined_bf, preferred_element_type=jnp.float32
        )
        real_parts.append((unitary * with_cos).astype(jnp.bfloat16))
        imag_parts.append((-unitary * with_sin).astype(jnp.bfloat16))
    spectra = jnp.stack([jnp.concatenate(real_parts, 1), jnp.concatenate(imag_parts, 1)])
    columns = lax.all_to_all(spectra, "slab", split_axis=2, concat_axis=3, tiled=True)
    payload = jnp.stack(
        [(vis_column * grid_size + vis_row).astype(jnp.float32), vis_real, vis_imag, vis_weight]
    )
    rank_size = math.gcd(rank_rows, vis_count)
    lower = (jnp.arange(rank_size)[:, None] > jnp.arange(rank_size)[None, :]).astype(jnp.float32)
    owner_hot = (owner_slab[:, None] == jnp.arange(slabs, dtype=jnp.int32)[None, :]).astype(
        jnp.float32
    )

    def rank_step(seen, hot_rows):
        before = jnp.dot(lower, hot_rows, precision=highest) + seen[None, :]
        return (seen + jnp.sum(hot_rows, 0), jnp.sum(before * hot_rows, 1))

    _, ranks = lax.scan(
        rank_step,
        jnp.zeros((slabs,), jnp.float32),
        owner_hot.reshape(vis_count // rank_size, rank_size, slabs),
    )
    destination = owner_slab * capacity + ranks.reshape(vis_count).astype(jnp.int32)
    buckets = (
        jnp.zeros((4, slabs * capacity), jnp.float32)
        .at[:, destination]
        .set(payload)
        .reshape(4, slabs, capacity)
    )
    arrived = lax.all_to_all(buckets, "slab", split_axis=1, concat_axis=1, tiled=True).reshape(
        4, slabs * capacity
    )
    span = walkers * owned
    flat = columns.reshape(2 * span, grid_size)
    total_slots = slabs * capacity
    step_rows = math.gcd(sample_rows, total_slots)
    owned_ids = jnp.arange(owned, dtype=jnp.int32)
    zeros_grid = jnp.zeros((span, grid_size), jnp.float32)

    def sample_step(index, sums):
        block_data = lax.dynamic_slice_in_dim(arrived, index * step_rows, step_rows, 1)
        cell_code = block_data[0].astype(jnp.int32)
        row_freq = cell_code % grid_size
        col_freq = cell_code // grid_size
        cos_rows, sin_rows = twiddle(row_freq, positions, grid_size)
        with_cos = lax.dot_general(
            cos_rows, flat, (((1,), (1,)), ((), ())), preferred_element_type=jnp.float32
        ).reshape(step_rows, 2, walkers, owned)
        with_sin = lax.dot_general(
            sin_rows, flat, (((1,), (1,)), ((), ())), preferred_element_type=jnp.float32
        ).reshape(step_rows, 2, walkers, owned)
        chooser = (col_freq[:, None] == owned_ids[None, :]).astype(jnp.float32)
        model_real = unitary * jnp.sum((with_cos[:, 0] + with_sin[:, 1]) * chooser[:, None, :], -1)
        model_imag = unitary * jnp.sum((with_cos[:, 1] - with_sin[:, 0]) * chooser[:, None, :], -1)
        error_real = (block_data[3][:, None] * (model_real - block_data[1][:, None])).astype(
            jnp.bfloat16
        )
        error_imag = (block_data[3][:, None] * (model_imag - block_data[2][:, None])).astype(
            jnp.bfloat16
        )
        spread = jnp.concatenate(
            [
                (error_real[:, :, None] * chooser[:, None, :]).reshape(step_rows, span),
                (error_imag[:, :, None] * chooser[:, None, :]).reshape(step_rows, span),
            ],
            1,
        ).astype(jnp.bfloat16)
        back_cos = lax.dot_general(
            spread, cos_rows, (((0,), (0,)), ((), ())), preferred_element_type=jnp.float32
        )
        back_sin = lax.dot_general(
            spread, sin_rows, (((0,), (0,)), ((), ())), preferred_element_type=jnp.float32
        )
        return (
            sums[0] + back_cos[:span] - back_sin[span:],
            sums[1] + back_sin[:span] + back_cos[span:],
        )

    sum_real, sum_imag = lax.fori_loop(
        0, total_slots // step_rows, sample_step, (zeros_grid, zeros_grid)
    )
    adjoint = (
        (unitary * jnp.stack([sum_real, sum_imag]))
        .astype(jnp.bfloat16)
        .reshape(2, walkers, owned, grid_size)
    )
    returned = lax.all_to_all(adjoint, "slab", split_axis=3, concat_axis=2, tiled=True)
    gradient = jnp.zeros((walkers, row_count, grid_size), jnp.float32)
    for offset in range(0, half_kx, step_kx):
        cos_rows, sin_rows = twiddle(
            offset + jnp.arange(step_kx, dtype=jnp.int32), positions, grid_size
        )
        part_real = returned[0][:, offset : offset + step_kx, :]
        part_imag = returned[1][:, offset : offset + step_kx, :]
        gradient = gradient + jnp.einsum(
            "wkr,kc->wrc", part_real, cos_rows, preferred_element_type=jnp.float32
        )
        gradient = gradient - jnp.einsum(
            "wkr,kc->wrc", part_imag, sin_rows, preferred_element_type=jnp.float32
        )
    gradient = unitary * gradient
    push_x = refract * slope_x[walkers][None] * gradient
    push_y = refract * slope_y[walkers][None] * gradient
    padded_y = with_halo(push_y.astype(jnp.bfloat16), (("slab", 1),), 2).astype(push_y.dtype)
    return col_adjoint(push_x) + row_adjoint(padded_y, row_count)


def solution(mesh):
    in_specs = (
        P(("chain", "vis"), "slab", None),
        P(("chain", "slab"), None),
        P("slab"),
        P("slab", None),
        P("slab"),
        P("slab"),
        P("slab"),
        P("slab"),
    )
    out_specs = P(("chain", "vis"), "slab", None)
    return jax.shard_map(local, mesh=mesh, in_specs=in_specs, out_specs=out_specs, check_vma=False)
```

profile of v0, /device:TPU:2, one launch (start us, length us, event | category | flops | bytes accessed | tf_op | source)
XLA Modules:
  0.0 358.0 jit_solution(11313475501157636354)
XLA Ops:
  4.5 13.8 %collective-permute-start.1 = (bf16[2,2,2048]{2,1,0:T(2,128)(2,1)S(1)}, bf16[2,2,2048]{2,1,0:T(2,128)(2,1)S(1)}, u32[]{:S(2)}, u32[]{:S(2)}) collective-permute-start(bf16[2,2,2048]{2,1,0:T(2,128)(2,1)S(1)} %get-tuple-element.290), channel_id=1, source_target_pairs={{2,0},{4,2},{6,4},{8,6},{10,8},{12,10},{14,12},{16,14},{18,16},{20... | collective-permute-start | bytes 49160 | tf_op jit(solution)/shard_map/ppermute | solution.py:22
  24.2 9.4 %all-to-all-start = ((f32[4,128,6]{2,0,1:T(4,128)}), f32[4,128,6]{2,0,1:T(4,128)S(1)}, u32[]{:S(2)}, u32[]{:S(2)}) async-start(f32[4,128,6]{2,0,1:T(4,128)} %copy.53), calls=%async_computation | async-start | bytes 524288 | tf_op jit(solution)/shard_map/all_to_all | solution.py:125
  34.5 8.8 %fusion.82 = bf16[1,256,16]{1,2,0:T(8,128)(2,1)S(1)} fusion(bf16[16,2048]{1,0:T(8,128)(2,1)S(1)} %fusion.111), kind=kOutput, calls=%fused_computation.142 | convolution fusion | flops 24649728 | bytes 73728 | tf_op jit(solution)/shard_map/kc,wrc->wkr/dot_general | solution.py:93
  43.3 8.1 %fusion.79 = bf16[1,256,16]{1,2,0:T(8,128)(2,1)S(1)} fusion(bf16[16,2048]{1,0:T(8,128)(2,1)S(1)} %fusion.111, s32[256]{0:T(256)S(1)} %iota_add_fusion), kind=kOutput, calls=%fused_computation.139 | convolution fusion | flops 24649728 | bytes 74752 | tf_op jit(solution)/shard_map/kc,wrc->wkr/dot_general | solution.py:93
  51.4 8.0 %fusion.83 = bf16[1,256,16]{1,2,0:T(8,128)(2,1)S(1)} fusion(bf16[16,2048]{1,0:T(8,128)(2,1)S(1)} %fusion.111, s32[256]{0:T(256)S(1)} %iota_add_fusion), kind=kOutput, calls=%fused_computation.143 | convolution fusion | flops 24649728 | bytes 74752 | tf_op jit(solution)/shard_map/kc,wrc->wkr/dot_general | solution.py:90
  59.4 8.6 %fusion.80 = bf16[1,256,16]{1,2,0:T(8,128)(2,1)S(1)} fusion(bf16[16,2048]{1,0:T(8,128)(2,1)S(1)} %fusion.111, s32[256]{0:T(256)S(1)} %iota_add_fusion.1), kind=kOutput, calls=%fused_computation.140 | convolution fusion | flops 24649728 | bytes 74752 | tf_op jit(solution)/shard_map/kc,wrc->wkr/dot_general | solution.py:93
  68.0 8.0 %fusion.84 = bf16[1,256,16]{1,2,0:T(8,128)(2,1)S(1)} fusion(bf16[16,2048]{1,0:T(8,128)(2,1)S(1)} %fusion.111, s32[256]{0:T(256)S(1)} %iota_add_fusion.1), kind=kOutput, calls=%fused_computation.144 | convolution fusion | flops 24649728 | bytes 74752 | tf_op jit(solution)/shard_map/kc,wrc->wkr/dot_general | solution.py:90
  76.0 8.3 %fusion.81 = bf16[1,256,16]{1,2,0:T(8,128)(2,1)S(1)} fusion(bf16[16,2048]{1,0:T(8,128)(2,1)S(1)} %fusion.111, s32[256]{0:T(256)S(1)} %iota_add_fusion.2), kind=kOutput, calls=%fused_computation.141 | convolution fusion | flops 24649728 | bytes 74752 | tf_op jit(solution)/shard_map/kc,wrc->wkr/dot_general | solution.py:93
  84.3 8.0 %fusion.85 = bf16[1,256,16]{1,2,0:T(8,128)(2,1)S(1)} fusion(bf16[16,2048]{1,0:T(8,128)(2,1)S(1)} %fusion.111, s32[256]{0:T(256)S(1)} %iota_add_fusion.2), kind=kOutput, calls=%fused_computation.145 | convolution fusion | flops 24649728 | bytes 74752 | tf_op jit(solution)/shard_map/kc,wrc->wkr/dot_general | solution.py:90
  92.3 8.7 %fusion.86 = bf16[1,256,16]{1,2,0:T(8,128)(2,1)S(1)} fusion(bf16[16,2048]{1,0:T(8,128)(2,1)S(1)} %fusion.111), kind=kOutput, calls=%fused_computation.146 | convolution fusion | flops 24649728 | bytes 73728 | tf_op jit(solution)/shard_map/kc,wrc->wkr/dot_general | solution.py:90
  102.5 16.4 %all-to-all-start.1 = ((bf16[128,2,128]{2,1,0:T(2,128)(2,1)}), bf16[128,2,128]{2,1,0:T(2,128)(2,1)S(1)}, u32[]{:S(2)}, u32[]{:S(2)}) async-start(bf16[128,2,128]{2,1,0:T(2,128)(2,1)} %reshape.696), calls=%async_computation.1 | async-start | bytes 131072 | tf_op jit(solution)/shard_map/all_to_all | solution.py:99
  119.1 14.1 %all-to-all-done.1 = bf16[128,2,128]{2,1,0:T(2,128)(2,1)S(1)} async-done(((bf16[128,2,128]{2,1,0:T(2,128)(2,1)}), bf16[128,2,128]{2,1,0:T(2,128)(2,1)S(1)}, u32[]{:S(2)}, u32[]{:S(2)}) %all-to-all-start.1) | async-done | bytes 65568 | tf_op jit(solution)/shard_map/all_to_all | solution.py:99
  134.6 120.4 %while.24 = (s32[]{:T(128)}, f32[8,2048]{1,0:T(8,128)S(1)}, f32[8,2048]{1,0:T(8,128)S(1)}, f32[4,768]{1,0:T(4,128)S(1)}, bf16[16,2048]{1,0:T(8,128)(2,1)S(1)}, /...) while((s32[]{:T(128)}, f32[8,2048]{1,0:T(8,128)S(1)}, ...), condition=%wide.region_5.6_spmd.clone.clone, body=%wide.region_2.5_spmd.clone.clone.sunk | while | flops 98724360 | bytes 1034473 | solution.py:174
  156.4 7.8 %fusion.213 = f32[256,16]{0,1:T(8,128)S(1)} fusion(bf16[16,2048]{1,0:T(8,128)(2,1)S(1)} %get-tuple-element.382, s32[256]{0:T(256)S(1)} %get-tuple-element.341), kind=kOutput, calls=%fused_computation.16.clone.1 | convolution fusion | flops 24641536 | bytes 82944 | tf_op jit(solution)/shard_map/while/body/eval_jaxpr/dot_general | solution.py:141
  164.3 7.9 %fusion.212 = f32[256,16]{0,1:T(8,128)S(1)} fusion(bf16[16,2048]{1,0:T(8,128)(2,1)S(1)} %get-tuple-element.382, s32[256]{0:T(256)S(1)} %get-tuple-element.341), kind=kOutput, calls=%fused_computation.18.clone.1 | convolution fusion | flops 24641536 | bytes 82944 | tf_op jit(solution)/shard_map/while/body/eval_jaxpr/dot_general | solution.py:144
  172.2 7.9 %fusion.218 = f32[16,2048]{1,0:T(8,128)S(1)} fusion(s32[256]{0:T(256)S(1)} %get-tuple-element.341, bf16[256,8]{0,1:T(8,128)(2,1)S(1)} %get-tuple-element.350, bf16[256,8]{0,1:T(8,128)(2,1)S(1)} %get-tuple-element.351), kind=kOutput, calls=%fused_computation.17.clone.1 | convolution fusion | flops 24657920 | bytes 140288 | tf_op jit(solution)/shard_map/while/body/eval_jaxpr/dot_general | solution.py:166
  180.1 7.8 %fusion.217 = f32[16,2048]{1,0:T(8,128)S(1)} fusion(s32[256]{0:T(256)S(1)} %get-tuple-element.341, bf16[256,8]{0,1:T(8,128)(2,1)S(1)} %get-tuple-element.350, bf16[256,8]{0,1:T(8,128)(2,1)S(1)} %get-tuple-element.351), kind=kOutput, calls=%fused_computation.15.clone.1 | convolution fusion | flops 24657920 | bytes 140288 | tf_op jit(solution)/shard_map/while/body/eval_jaxpr/dot_general | solution.py:163
  188.1 7.8 %fusion.213 = f32[256,16]{0,1:T(8,128)S(1)} fusion(bf16[16,2048]{1,0:T(8,128)(2,1)S(1)} %get-tuple-element.382, s32[256]{0:T(256)S(1)} %get-tuple-element.341), kind=kOutput, calls=%fused_computation.16.clone.1 | convolution fusion | flops 24641536 | bytes 82944 | tf_op jit(solution)/shard_map/while/body/eval_jaxpr/dot_general | solution.py:141
  195.9 7.9 %fusion.212 = f32[256,16]{0,1:T(8,128)S(1)} fusion(bf16[16,2048]{1,0:T(8,128)(2,1)S(1)} %get-tuple-element.382, s32[256]{0:T(256)S(1)} %get-tuple-element.341), kind=kOutput, calls=%fused_computation.18.clone.1 | convolution fusion | flops 24641536 | bytes 82944 | tf_op jit(solution)/shard_map/while/body/eval_jaxpr/dot_general | solution.py:144
  203.9 7.9 %fusion.218 = f32[16,2048]{1,0:T(8,128)S(1)} fusion(s32[256]{0:T(256)S(1)} %get-tuple-element.341, bf16[256,8]{0,1:T(8,128)(2,1)S(1)} %get-tuple-element.350, bf16[256,8]{0,1:T(8,128)(2,1)S(1)} %get-tuple-element.351), kind=kOutput, calls=%fused_computation.17.clone.1 | convolution fusion | flops 24657920 | bytes 140288 | tf_op jit(solution)/shard_map/while/body/eval_jaxpr/dot_general | solution.py:166
  211.8 7.8 %fusion.217 = f32[16,2048]{1,0:T(8,128)S(1)} fusion(s32[256]{0:T(256)S(1)} %get-tuple-element.341, bf16[256,8]{0,1:T(8,128)(2,1)S(1)} %get-tuple-element.350, bf16[256,8]{0,1:T(8,128)(2,1)S(1)} %get-tuple-element.351), kind=kOutput, calls=%fused_computation.15.clone.1 | convolution fusion | flops 24657920 | bytes 140288 | tf_op jit(solution)/shard_map/while/body/eval_jaxpr/dot_general | solution.py:163
  219.8 7.8 %fusion.213 = f32[256,16]{0,1:T(8,128)S(1)} fusion(bf16[16,2048]{1,0:T(8,128)(2,1)S(1)} %get-tuple-element.382, s32[256]{0:T(256)S(1)} %get-tuple-element.341), kind=kOutput, calls=%fused_computation.16.clone.1 | convolution fusion | flops 24641536 | bytes 82944 | tf_op jit(solution)/shard_map/while/body/eval_jaxpr/dot_general | solution.py:141
  227.6 7.9 %fusion.212 = f32[256,16]{0,1:T(8,128)S(1)} fusion(bf16[16,2048]{1,0:T(8,128)(2,1)S(1)} %get-tuple-element.382, s32[256]{0:T(256)S(1)} %get-tuple-element.341), kind=kOutput, calls=%fused_computation.18.clone.1 | convolution fusion | flops 24641536 | bytes 82944 | tf_op jit(solution)/shard_map/while/body/eval_jaxpr/dot_general | solution.py:144
  235.6 7.9 %fusion.218 = f32[16,2048]{1,0:T(8,128)S(1)} fusion(s32[256]{0:T(256)S(1)} %get-tuple-element.341, bf16[256,8]{0,1:T(8,128)(2,1)S(1)} %get-tuple-element.350, bf16[256,8]{0,1:T(8,128)(2,1)S(1)} %get-tuple-element.351), kind=kOutput, calls=%fused_computation.17.clone.1 | convolution fusion | flops 24657920 | bytes 140288 | tf_op jit(solution)/shard_map/while/body/eval_jaxpr/dot_general | solution.py:166
  256.8 19.9 %all_to_all.35 = bf16[128,2,128]{2,1,0:T(2,128)(2,1)S(1)} all-to-all(bf16[128,2,128]{2,1,0:T(2,128)(2,1)S(1)} %reshape.698), channel_id=1, replica_groups=mesh['chain'=2,'slab'=128,'vis'=2] {'slab'}, dimensions={0} | all-to-all | bytes 131072 | tf_op jit(solution)/shard_map/all_to_all | solution.py:182
  287.5 8.2 %convolution_subtract_fusion.3 = f32[16,2048]{1,0:T(8,128)S(1)} fusion(f32[16,2048]{1,0:T(8,128)S(1)} %fusion.87, bf16[1,1024,16]{2,1,0:T(8,128)(2,1)S(1)} %bitcast.172), kind=kOutput, calls=%fused_computation.88 | convolution fusion | flops 24674304 | bytes 327680 | tf_op jit(solution)/shard_map/wkr,kc->wrc/dot_general | solution.py:193
  295.7 8.0 %convolution_add_fusion.2 = f32[16,2048]{1,0:T(8,128)S(1)} fusion(f32[16,2048]{1,0:T(8,128)S(1)} %convolution_subtract_fusion.3, s32[256]{0:T(256)S(1)} %iota_add_fusion.2, bf16[1,1024,16]{2,1,0:T(8,128)(2,1)S(1)} %bitcast.177), kind=kOutput, calls=%fused_computation.87 | convolution fusion | flops 24674304 | bytes 328704 | tf_op jit(solution)/shard_map/wkr,kc->wrc/dot_general | solution.py:190
  303.7 7.9 %convolution_subtract_fusion.2 = f32[16,2048]{1,0:T(8,128)S(1)} fusion(f32[16,2048]{1,0:T(8,128)S(1)} %convolution_add_fusion.2, s32[256]{0:T(256)S(1)} %iota_add_fusion.2, bf16[1,1024,16]{2,1,0:T(8,128)(2,1)S(1)} %bitcast.173), kind=kOutput, calls=%fused_computation.86 | convolution fusion | flops 24674304 | bytes 328704 | tf_op jit(solution)/shard_map/wkr,kc->wrc/dot_general | solution.py:193
  311.6 8.0 %convolution_add_fusion.1 = f32[16,2048]{1,0:T(8,128)S(1)} fusion(f32[16,2048]{1,0:T(8,128)S(1)} %convolution_subtract_fusion.2, s32[256]{0:T(256)S(1)} %iota_add_fusion.1, bf16[1,1024,16]{2,1,0:T(8,128)(2,1)S(1)} %bitcast.178), kind=kOutput, calls=%fused_computation.85 | convolution fusion | flops 24674304 | bytes 328704 | tf_op jit(solution)/shard_map/wkr,kc->wrc/dot_general | solution.py:190
  319.6 8.3 %convolution_subtract_fusion.1 = f32[16,2048]{1,0:T(8,128)S(1)} fusion(f32[16,2048]{1,0:T(8,128)S(1)} %convolution_add_fusion.1, s32[256]{0:T(256)S(1)} %iota_add_fusion.1, bf16[1,1024,16]{2,1,0:T(8,128)(2,1)S(1)} %bitcast.174), kind=kOutput, calls=%fused_computation.84 | convolution fusion | flops 24674304 | bytes 328704 | tf_op jit(solution)/shard_map/wkr,kc->wrc/dot_general | solution.py:193
  335.6 8.1 %slice_multiply_fusion.2 = (f32[1,16,2048]{2,1,0:T(8,128)S(1)}, bf16[1,16,2048]{2,1,0:T(8,128)(2,1)S(1)}) fusion(f32[2,16,2048]{2,1,0:T(8,128)S(1)} %fusion.98, f32[2,16,2048]{2,1,0:T(8,128)S(1)} %fusion.94, f32[16,2048]{1,0:T(8,128)S(1)} %convolution_add_fusion, s32[256]{0:T(256)S(1)} %iota_add_fusion, bf16[1,1024,16]{2,1,0:T(8,128)(2,1)S(1)} %bitcast.175), kind=kOutput, calls=%fused_computation.206 | convolution fusion | flops 24805376 | bytes 656384 | tf_op jit(solution)/shard_map/wkr,kc->wrc/dot_general | solution.py:193
  346.6 9.0 %collective-permute-start.3 = (bf16[1,2,2048]{2,1,0:T(2,128)(2,1)S(1)}, bf16[1,2,2048]{2,1,0:T(2,128)(2,1)S(1)}, u32[]{:S(2)}, u32[]{:S(2)}) collective-permute-start(bf16[1,2,2048]{2,1,0:T(2,128)(2,1)S(1)} %get-tuple-element.292), channel_id=1, source_target_pairs={{2,0},{4,2},{6,4},{8,6},{10,8},{12,10},{14,12},{16,14},{18,16},{20... | collective-permute-start | bytes 24584 | tf_op jit(solution)/shard_map/ppermute | solution.py:22
  (82 shorter events, 47.7 us)
Async XLA Ops:
  1.0 33.2 %collective-permute-start = (bf16[2,2,2048]{2,1,0:T(2,128)(2,1)S(1)}, bf16[2,2,2048]{2,1,0:T(2,128)(2,1)S(1)}, u32[]{:S(2)}, u32[]{:S(2)}) collective-permute-start(bf16[2,2,2048]{2,1,0:T(2,128)(2,1)S(1)} %get-tuple-element.289), channel_id=1, source_target_pairs={{0,2},{2,4},{4,6},{6,8},{8,10},{10,12},{12,14},{14,16},{16,18},{18... | collective-permute-start | bytes 49160 | tf_op jit(solution)/shard_map/ppermute | solution.py:20
  4.5 29.8 %collective-permute-start.1 = (bf16[2,2,2048]{2,1,0:T(2,128)(2,1)S(1)}, bf16[2,2,2048]{2,1,0:T(2,128)(2,1)S(1)}, u32[]{:S(2)}, u32[]{:S(2)}) collective-permute-start(bf16[2,2,2048]{2,1,0:T(2,128)(2,1)S(1)} %get-tuple-element.290), channel_id=1, source_target_pairs={{2,0},{4,2},{6,4},{8,6},{10,8},{12,10},{14,12},{16,14},{18,16},{20... | collective-permute-start | bytes 49160 | tf_op jit(solution)/shard_map/ppermute | solution.py:22
  21.6 11.9 %copy-start = (f32[16,2048]{1,0:T(8,128)S(1)}, f32[16,2048]{1,0:T(8,128)}, u32[]{:S(2)}) copy-start(f32[16,2048]{1,0:T(8,128)} %param.11) | copy-start | bytes 393220
  21.6 11.9 %copy-start.1 = (f32[1,16,2048]{2,1,0:T(8,128)S(1)}, f32[1,16,2048]{2,1,0:T(8,128)}, u32[]{:S(2)}) copy-start(f32[1,16,2048]{2,1,0:T(8,128)} %param.10) | copy-start | bytes 393220
  24.2 78.3 %all-to-all-start = ((f32[4,128,6]{2,0,1:T(4,128)}), f32[4,128,6]{2,0,1:T(4,128)S(1)}, u32[]{:S(2)}, u32[]{:S(2)}) async-start(f32[4,128,6]{2,0,1:T(4,128)} %copy.53), calls=%async_computation | async-start | bytes 524288 | tf_op jit(solution)/shard_map/all_to_all | solution.py:125
  102.5 30.8 %all-to-all-start.1 = ((bf16[128,2,128]{2,1,0:T(2,128)(2,1)}), bf16[128,2,128]{2,1,0:T(2,128)(2,1)S(1)}, u32[]{:S(2)}, u32[]{:S(2)}) async-start(bf16[128,2,128]{2,1,0:T(2,128)(2,1)} %reshape.696), calls=%async_computation.1 | async-start | bytes 131072 | tf_op jit(solution)/shard_map/all_to_all | solution.py:99
  344.0 11.7 %collective-permute-start.2 = (bf16[1,2,2048]{2,1,0:T(2,128)(2,1)S(1)}, bf16[1,2,2048]{2,1,0:T(2,128)(2,1)S(1)}, u32[]{:S(2)}, u32[]{:S(2)}) collective-permute-start(bf16[1,2,2048]{2,1,0:T(2,128)(2,1)S(1)} %get-tuple-element.291), channel_id=1, source_target_pairs={{0,2},{2,4},{4,6},{6,8},{8,10},{10,12},{12,14},{14,16},{16,18},{18... | collective-permute-start | bytes 24584 | tf_op jit(solution)/shard_map/ppermute | solution.py:20
  346.6 10.4 %collective-permute-start.3 = (bf16[1,2,2048]{2,1,0:T(2,128)(2,1)S(1)}, bf16[1,2,2048]{2,1,0:T(2,128)(2,1)S(1)}, u32[]{:S(2)}, u32[]{:S(2)}) collective-permute-start(bf16[1,2,2048]{2,1,0:T(2,128)(2,1)S(1)} %get-tuple-element.292), channel_id=1, source_target_pairs={{2,0},{4,2},{6,4},{8,6},{10,8},{12,10},{14,12},{16,14},{18,16},{20... | collective-permute-start | bytes 24584 | tf_op jit(solution)/shard_map/ppermute | solution.py:22
where the time goes:
time: 361 us; the launch traced here: 358 us
  matrix products  226 us (63%)
  starting transfers between devices  54.7 us (15%)
  loops' own time  25.6 us (7%)
  blocking collectives  19.9 us (6%)
  waiting for transfers between devices  15.4 us (4%)
  local copies, waits for them, and re-layouts  10.7 us (3%)
  other arithmetic  5.4 us (1%)
    dot_general x4, matrix products, local(): jnp.einsum('kc,wrc->wkr', sin_rows, joined_bf, preferred_element_type=jnp...  33.7 us
    dot_general x4, matrix products, local(): jnp.einsum('kc,wrc->wkr', cos_rows, joined_bf, preferred_element_type=jnp...  32.8 us
    dot_general x4, matrix products, local(): jnp.einsum('wkr,kc->wrc', part_imag, sin_rows, preferred_element_type=jnp...  32.4 us
    dot_general x4, matrix products, local(): jnp.einsum('wkr,kc->wrc', part_real, cos_rows, preferred_element_type=jnp...  31.5 us
    another operation x1, loops' own time, local(): lax.fori_loop(0, total_slots // step_rows, sample_step, (zeros_grid, zero...  25.6 us
    dot_general x3, matrix products, sample_step(): lax.dot_general(sin_rows, flat, (((1,), (1,)), ((), ())), preferred_eleme...  23.8 us
    dot_general x3, matrix products, sample_step(): lax.dot_general(spread, sin_rows, (((0,), (0,)), ((), ())), preferred_ele...  23.6 us
    dot_general x3, matrix products, sample_step(): lax.dot_general(cos_rows, flat, (((1,), (1,)), ((), ())), preferred_eleme...  23.5 us
  transfers between devices with their start and end apart: 6, of which 2 were waited for; matrix products, arithmetic and copies ran while one was open for 21% of the time, Pallas kernels for 0%

commit v1 on v0

--- a/solution.py
+++ b/solution.py
@@ -8,6 +8,15 @@
 rank_rows = 512
 sample_rows = 256
 table_rows = 256
+use_heaps_for = lambda x_in, mesh_dim, dim_i, at_axis: jnp.concatenate(
+    lax.all_to_all(
+        jnp.stack(jnp.split(x_in, lax.axis_size(mesh_dim), axis=dim_i), axis=0),
+        axis_name=mesh_dim,
+        split_axis=0,
+        concat_axis=0,
+    ),
+    axis=at_axis,
+)
 
 
 def with_halo(cells, sides, width):
@@ -122,9 +131,7 @@
         .set(payload)
         .reshape(4, slabs, capacity)
     )
-    arrived = lax.all_to_all(buckets, "slab", split_axis=1, concat_axis=1, tiled=True).reshape(
-        4, slabs * capacity
-    )
+    arrived = use_heaps_for(buckets, "slab", 1, 1).reshape(4, slabs * capacity)
     span = walkers * owned
     flat = columns.reshape(2 * span, grid_size)
     total_slots = slabs * capacity

time: 361 us -> 436 us (1.21)
  local copies, waits for them, and re-layouts: 10.7 us -> 84.3 us
    unnamed x8 -> x135, local copies, waits for them, and re-layouts: 3.58 us -> 77.2 us
  transfers between devices with their start and end apart: 6 -> 6, of which waited for: 2 -> 2; matrix products, arithmetic and copies ran while one was open for 21% -> 34% of each run, Pallas kernels for 0% -> 0%
where the time goes in v1:
time: 436 us; the launch traced here: 432 us
  matrix products  226 us (52%)
  local copies, waits for them, and re-layouts  84.3 us (19%)
  starting transfers between devices  54.7 us (13%)
  loops' own time  25.6 us (6%)
  blocking collectives  19.9 us (5%)
  waiting for transfers between devices  15.4 us (4%)
  other arithmetic  5.4 us (1%)
    unnamed x135, local copies, waits for them, and re-layouts  77.2 us
    dot_general x4, matrix products, local(): jnp.einsum('kc,wrc->wkr', sin_rows, joined_bf, preferred_element_type=jnp...  33.7 us
    dot_general x4, matrix products, local(): jnp.einsum('kc,wrc->wkr', cos_rows, joined_bf, preferred_element_type=jnp...  32.8 us
    dot_general x4, matrix products, local(): jnp.einsum('wkr,kc->wrc', part_imag, sin_rows, preferred_element_type=jnp...  32.4 us
    dot_general x4, matrix products, local(): jnp.einsum('wkr,kc->wrc', part_real, cos_rows, preferred_element_type=jnp...  31.5 us
    another operation x1, loops' own time, local(): lax.fori_loop(0, total_slots // step_rows, sample_step, (zeros_grid, zero...  25.6 us
    dot_general x3, matrix products, sample_step(): lax.dot_general(sin_rows, flat, (((1,), (1,)), ((), ())), preferred_eleme...  23.8 us
    dot_general x3, matrix products, sample_step(): lax.dot_general(spread, sin_rows, (((0,), (0,)), ((), ())), preferred_ele...  23.6 us
  transfers between devices with their start and end apart: 6, of which 2 were waited for; matrix products, arithmetic and copies ran while one was open for 34% of the time, Pallas kernels for 0%

profile of v1, /device:TPU:2, one launch (start us, length us, event | category | flops | bytes accessed | tf_op | source)
XLA Modules:
  0.0 431.7 jit_solution(9069171801829583658)
XLA Ops:
  4.5 13.8 %collective-permute-start.1 = (bf16[2,2,2048]{2,1,0:T(2,128)(2,1)S(1)}, bf16[2,2,2048]{2,1,0:T(2,128)(2,1)S(1)}, u32[]{:S(2)}, u32[]{:S(2)}) collective-permute-start(bf16[2,2,2048]{2,1,0:T(2,128)(2,1)S(1)} %get-tuple-element.418), channel_id=1, source_target_pairs={{2,0},{4,2},{6,4},{8,6},{10,8},{12,10},{14,12},{16,14},{18,16},{20... | collective-permute-start | bytes 49160 | tf_op jit(solution)/shard_map/ppermute | solution.py:31
  97.9 9.4 %all-to-all-start = ((f32[128,4,1,6]{3,1,2,0:T(4,128)}), f32[128,4,1,6]{3,1,2,0:T(4,128)S(1)}, u32[]{:S(2)}, u32[]{:S(2)}) async-start(f32[128,4,1,6]{3,1,2,0:T(4,128)} %constant_dynamic-update-slice_fusion), calls=%async_computation | async-start | bytes 524288 | tf_op jit(solution)/shard_map/all_to_all | solution.py:12
  108.2 8.8 %fusion.82 = bf16[1,256,16]{1,2,0:T(8,128)(2,1)S(1)} fusion(bf16[16,2048]{1,0:T(8,128)(2,1)S(1)} %fusion.111), kind=kOutput, calls=%fused_computation.142 | convolution fusion | flops 24649728 | bytes 73728 | tf_op jit(solution)/shard_map/kc,wrc->wkr/dot_general | solution.py:102
  117.0 8.1 %fusion.79 = bf16[1,256,16]{1,2,0:T(8,128)(2,1)S(1)} fusion(bf16[16,2048]{1,0:T(8,128)(2,1)S(1)} %fusion.111, s32[256]{0:T(256)S(1)} %iota_add_fusion), kind=kOutput, calls=%fused_computation.139 | convolution fusion | flops 24649728 | bytes 74752 | tf_op jit(solution)/shard_map/kc,wrc->wkr/dot_general | solution.py:102
  125.1 8.0 %fusion.83 = bf16[1,256,16]{1,2,0:T(8,128)(2,1)S(1)} fusion(bf16[16,2048]{1,0:T(8,128)(2,1)S(1)} %fusion.111, s32[256]{0:T(256)S(1)} %iota_add_fusion), kind=kOutput, calls=%fused_computation.143 | convolution fusion | flops 24649728 | bytes 74752 | tf_op jit(solution)/shard_map/kc,wrc->wkr/dot_general | solution.py:99
  133.1 8.6 %fusion.80 = bf16[1,256,16]{1,2,0:T(8,128)(2,1)S(1)} fusion(bf16[16,2048]{1,0:T(8,128)(2,1)S(1)} %fusion.111, s32[256]{0:T(256)S(1)} %iota_add_fusion.1), kind=kOutput, calls=%fused_computation.140 | convolution fusion | flops 24649728 | bytes 74752 | tf_op jit(solution)/shard_map/kc,wrc->wkr/dot_general | solution.py:102
  141.7 8.0 %fusion.84 = bf16[1,256,16]{1,2,0:T(8,128)(2,1)S(1)} fusion(bf16[16,2048]{1,0:T(8,128)(2,1)S(1)} %fusion.111, s32[256]{0:T(256)S(1)} %iota_add_fusion.1), kind=kOutput, calls=%fused_computation.144 | convolution fusion | flops 24649728 | bytes 74752 | tf_op jit(solution)/shard_map/kc,wrc->wkr/dot_general | solution.py:99
  149.7 8.3 %fusion.81 = bf16[1,256,16]{1,2,0:T(8,128)(2,1)S(1)} fusion(bf16[16,2048]{1,0:T(8,128)(2,1)S(1)} %fusion.111, s32[256]{0:T(256)S(1)} %iota_add_fusion.2), kind=kOutput, calls=%fused_computation.141 | convolution fusion | flops 24649728 | bytes 74752 | tf_op jit(solution)/shard_map/kc,wrc->wkr/dot_general | solution.py:102
  158.0 8.0 %fusion.85 = bf16[1,256,16]{1,2,0:T(8,128)(2,1)S(1)} fusion(bf16[16,2048]{1,0:T(8,128)(2,1)S(1)} %fusion.111, s32[256]{0:T(256)S(1)} %iota_add_fusion.2), kind=kOutput, calls=%fused_computation.145 | convolution fusion | flops 24649728 | bytes 74752 | tf_op jit(solution)/shard_map/kc,wrc->wkr/dot_general | solution.py:99
  166.1 8.7 %fusion.86 = bf16[1,256,16]{1,2,0:T(8,128)(2,1)S(1)} fusion(bf16[16,2048]{1,0:T(8,128)(2,1)S(1)} %fusion.111), kind=kOutput, calls=%fused_computation.146 | convolution fusion | flops 24649728 | bytes 73728 | tf_op jit(solution)/shard_map/kc,wrc->wkr/dot_general | solution.py:99
  176.2 16.4 %all-to-all-start.1 = ((bf16[128,2,128]{2,1,0:T(2,128)(2,1)}), bf16[128,2,128]{2,1,0:T(2,128)(2,1)S(1)}, u32[]{:S(2)}, u32[]{:S(2)}) async-start(bf16[128,2,128]{2,1,0:T(2,128)(2,1)} %reshape.696), calls=%async_computation.1 | async-start | bytes 131072 | tf_op jit(solution)/shard_map/all_to_all | solution.py:108
  192.8 14.1 %all-to-all-done.1 = bf16[128,2,128]{2,1,0:T(2,128)(2,1)S(1)} async-done(((bf16[128,2,128]{2,1,0:T(2,128)(2,1)}), bf16[128,2,128]{2,1,0:T(2,128)(2,1)S(1)}, u32[]{:S(2)}, u32[]{:S(2)}) %all-to-all-start.1) | async-done | bytes 65568 | tf_op jit(solution)/shard_map/all_to_all | solution.py:108
  208.3 120.4 %while.24 = (s32[]{:T(128)}, f32[8,2048]{1,0:T(8,128)S(1)}, f32[8,2048]{1,0:T(8,128)S(1)}, f32[4,768]{1,0:T(4,128)S(1)}, bf16[16,2048]{1,0:T(8,128)(2,1)S(1)}, /...) while((s32[]{:T(128)}, f32[8,2048]{1,0:T(8,128)S(1)}, ...), condition=%wide.region_5.6_spmd.clone.clone, body=%wide.region_2.5_spmd.clone.clone.sunk | while | flops 98724360 | bytes 1034473 | solution.py:181
  230.1 7.8 %fusion.220 = f32[256,16]{0,1:T(8,128)S(1)} fusion(bf16[16,2048]{1,0:T(8,128)(2,1)S(1)} %get-tuple-element.510, s32[256]{0:T(256)S(1)} %get-tuple-element.469), kind=kOutput, calls=%fused_computation.16.clone.1 | convolution fusion | flops 24641536 | bytes 82944 | tf_op jit(solution)/shard_map/while/body/eval_jaxpr/dot_general | solution.py:148
  238.0 7.9 %fusion.219 = f32[256,16]{0,1:T(8,128)S(1)} fusion(bf16[16,2048]{1,0:T(8,128)(2,1)S(1)} %get-tuple-element.510, s32[256]{0:T(256)S(1)} %get-tuple-element.469), kind=kOutput, calls=%fused_computation.18.clone.1 | convolution fusion | flops 24641536 | bytes 82944 | tf_op jit(solution)/shard_map/while/body/eval_jaxpr/dot_general | solution.py:151
  246.0 7.9 %fusion.225 = f32[16,2048]{1,0:T(8,128)S(1)} fusion(s32[256]{0:T(256)S(1)} %get-tuple-element.469, bf16[256,8]{0,1:T(8,128)(2,1)S(1)} %get-tuple-element.478, bf16[256,8]{0,1:T(8,128)(2,1)S(1)} %get-tuple-element.479), kind=kOutput, calls=%fused_computation.17.clone.1 | convolution fusion | flops 24657920 | bytes 140288 | tf_op jit(solution)/shard_map/while/body/eval_jaxpr/dot_general | solution.py:173
  253.8 7.8 %fusion.224 = f32[16,2048]{1,0:T(8,128)S(1)} fusion(s32[256]{0:T(256)S(1)} %get-tuple-element.469, bf16[256,8]{0,1:T(8,128)(2,1)S(1)} %get-tuple-element.478, bf16[256,8]{0,1:T(8,128)(2,1)S(1)} %get-tuple-element.479), kind=kOutput, calls=%fused_computation.15.clone.1 | convolution fusion | flops 24657920 | bytes 140288 | tf_op jit(solution)/shard_map/while/body/eval_jaxpr/dot_general | solution.py:170
  261.8 7.8 %fusion.220 = f32[256,16]{0,1:T(8,128)S(1)} fusion(bf16[16,2048]{1,0:T(8,128)(2,1)S(1)} %get-tuple-element.510, s32[256]{0:T(256)S(1)} %get-tuple-element.469), kind=kOutput, calls=%fused_computation.16.clone.1 | convolution fusion | flops 24641536 | bytes 82944 | tf_op jit(solution)/shard_map/while/body/eval_jaxpr/dot_general | solution.py:148
  269.6 7.9 %fusion.219 = f32[256,16]{0,1:T(8,128)S(1)} fusion(bf16[16,2048]{1,0:T(8,128)(2,1)S(1)} %get-tuple-element.510, s32[256]{0:T(256)S(1)} %get-tuple-element.469), kind=kOutput, calls=%fused_computation.18.clone.1 | convolution fusion | flops 24641536 | bytes 82944 | tf_op jit(solution)/shard_map/while/body/eval_jaxpr/dot_general | solution.py:151
  277.6 7.9 %fusion.225 = f32[16,2048]{1,0:T(8,128)S(1)} fusion(s32[256]{0:T(256)S(1)} %get-tuple-element.469, bf16[256,8]{0,1:T(8,128)(2,1)S(1)} %get-tuple-element.478, bf16[256,8]{0,1:T(8,128)(2,1)S(1)} %get-tuple-element.479), kind=kOutput, calls=%fused_computation.17.clone.1 | convolution fusion | flops 24657920 | bytes 140288 | tf_op jit(solution)/shard_map/while/body/eval_jaxpr/dot_general | solution.py:173
  285.5 7.8 %fusion.224 = f32[16,2048]{1,0:T(8,128)S(1)} fusion(s32[256]{0:T(256)S(1)} %get-tuple-element.469, bf16[256,8]{0,1:T(8,128)(2,1)S(1)} %get-tuple-element.478, bf16[256,8]{0,1:T(8,128)(2,1)S(1)} %get-tuple-element.479), kind=kOutput, calls=%fused_computation.15.clone.1 | convolution fusion | flops 24657920 | bytes 140288 | tf_op jit(solution)/shard_map/while/body/eval_jaxpr/dot_general | solution.py:170
  293.5 7.8 %fusion.220 = f32[256,16]{0,1:T(8,128)S(1)} fusion(bf16[16,2048]{1,0:T(8,128)(2,1)S(1)} %get-tuple-element.510, s32[256]{0:T(256)S(1)} %get-tuple-element.469), kind=kOutput, calls=%fused_computation.16.clone.1 | convolution fusion | flops 24641536 | bytes 82944 | tf_op jit(solution)/shard_map/while/body/eval_jaxpr/dot_general | solution.py:148
  301.3 7.9 %fusion.219 = f32[256,16]{0,1:T(8,128)S(1)} fusion(bf16[16,2048]{1,0:T(8,128)(2,1)S(1)} %get-tuple-element.510, s32[256]{0:T(256)S(1)} %get-tuple-element.469), kind=kOutput, calls=%fused_computation.18.clone.1 | convolution fusion | flops 24641536 | bytes 82944 | tf_op jit(solution)/shard_map/while/body/eval_jaxpr/dot_general | solution.py:151
  309.3 7.9 %fusion.225 = f32[16,2048]{1,0:T(8,128)S(1)} fusion(s32[256]{0:T(256)S(1)} %get-tuple-element.469, bf16[256,8]{0,1:T(8,128)(2,1)S(1)} %get-tuple-element.478, bf16[256,8]{0,1:T(8,128)(2,1)S(1)} %get-tuple-element.479), kind=kOutput, calls=%fused_computation.17.clone.1 | convolution fusion | flops 24657920 | bytes 140288 | tf_op jit(solution)/shard_map/while/body/eval_jaxpr/dot_general | solution.py:173
  330.6 19.9 %all_to_all.35 = bf16[128,2,128]{2,1,0:T(2,128)(2,1)S(1)} all-to-all(bf16[128,2,128]{2,1,0:T(2,128)(2,1)S(1)} %reshape.698), channel_id=1, replica_groups=mesh['chain'=2,'slab'=128,'vis'=2] {'slab'}, dimensions={0} | all-to-all | bytes 131072 | tf_op jit(solution)/shard_map/all_to_all | solution.py:189
  361.2 8.2 %convolution_subtract_fusion.3 = f32[16,2048]{1,0:T(8,128)S(1)} fusion(f32[16,2048]{1,0:T(8,128)S(1)} %fusion.87, bf16[1,1024,16]{2,1,0:T(8,128)(2,1)S(1)} %bitcast.306), kind=kOutput, calls=%fused_computation.88 | convolution fusion | flops 24674304 | bytes 327680 | tf_op jit(solution)/shard_map/wkr,kc->wrc/dot_general | solution.py:200
  369.4 8.0 %convolution_add_fusion.2 = f32[16,2048]{1,0:T(8,128)S(1)} fusion(f32[16,2048]{1,0:T(8,128)S(1)} %convolution_subtract_fusion.3, s32[256]{0:T(256)S(1)} %iota_add_fusion.2, bf16[1,1024,16]{2,1,0:T(8,128)(2,1)S(1)} %bitcast.311), kind=kOutput, calls=%fused_computation.87 | convolution fusion | flops 24674304 | bytes 328704 | tf_op jit(solution)/shard_map/wkr,kc->wrc/dot_general | solution.py:197
  377.4 7.9 %convolution_subtract_fusion.2 = f32[16,2048]{1,0:T(8,128)S(1)} fusion(f32[16,2048]{1,0:T(8,128)S(1)} %convolution_add_fusion.2, s32[256]{0:T(256)S(1)} %iota_add_fusion.2, bf16[1,1024,16]{2,1,0:T(8,128)(2,1)S(1)} %bitcast.307), kind=kOutput, calls=%fused_computation.86 | convolution fusion | flops 24674304 | bytes 328704 | tf_op jit(solution)/shard_map/wkr,kc->wrc/dot_general | solution.py:200
  385.3 8.0 %convolution_add_fusion.1 = f32[16,2048]{1,0:T(8,128)S(1)} fusion(f32[16,2048]{1,0:T(8,128)S(1)} %convolution_subtract_fusion.2, s32[256]{0:T(256)S(1)} %iota_add_fusion.1, bf16[1,1024,16]{2,1,0:T(8,128)(2,1)S(1)} %bitcast.312), kind=kOutput, calls=%fused_computation.85 | convolution fusion | flops 24674304 | bytes 328704 | tf_op jit(solution)/shard_map/wkr,kc->wrc/dot_general | solution.py:197
  393.3 8.3 %convolution_subtract_fusion.1 = f32[16,2048]{1,0:T(8,128)S(1)} fusion(f32[16,2048]{1,0:T(8,128)S(1)} %convolution_add_fusion.1, s32[256]{0:T(256)S(1)} %iota_add_fusion.1, bf16[1,1024,16]{2,1,0:T(8,128)(2,1)S(1)} %bitcast.308), kind=kOutput, calls=%fused_computation.84 | convolution fusion | flops 24674304 | bytes 328704 | tf_op jit(solution)/shard_map/wkr,kc->wrc/dot_general | solution.py:200
  409.4 8.1 %slice_multiply_fusion.2 = (f32[1,16,2048]{2,1,0:T(8,128)S(1)}, bf16[1,16,2048]{2,1,0:T(8,128)(2,1)S(1)}) fusion(f32[2,16,2048]{2,1,0:T(8,128)S(1)} %fusion.98, f32[2,16,2048]{2,1,0:T(8,128)S(1)} %fusion.94, f32[16,2048]{1,0:T(8,128)S(1)} %convolution_add_fusion, s32[256]{0:T(256)S(1)} %iota_add_fusion, bf16[1,1024,16]{2,1,0:T(8,128)(2,1)S(1)} %bitcast.309), kind=kOutput, calls=%fused_computation.334 | convolution fusion | flops 24805376 | bytes 656384 | tf_op jit(solution)/shard_map/wkr,kc->wrc/dot_general | solution.py:200
  420.3 9.0 %collective-permute-start.3 = (bf16[1,2,2048]{2,1,0:T(2,128)(2,1)S(1)}, bf16[1,2,2048]{2,1,0:T(2,128)(2,1)S(1)}, u32[]{:S(2)}, u32[]{:S(2)}) collective-permute-start(bf16[1,2,2048]{2,1,0:T(2,128)(2,1)S(1)} %get-tuple-element.420), channel_id=1, source_target_pairs={{2,0},{4,2},{6,4},{8,6},{10,8},{12,10},{14,12},{16,14},{18,16},{20... | collective-permute-start | bytes 24584 | tf_op jit(solution)/shard_map/ppermute | solution.py:31
  (216 shorter events, 121.3 us)
Async XLA Ops:
  1.0 107.0 %collective-permute-start = (bf16[2,2,2048]{2,1,0:T(2,128)(2,1)S(1)}, bf16[2,2,2048]{2,1,0:T(2,128)(2,1)S(1)}, u32[]{:S(2)}, u32[]{:S(2)}) collective-permute-start(bf16[2,2,2048]{2,1,0:T(2,128)(2,1)S(1)} %get-tuple-element.417), channel_id=1, source_target_pairs={{0,2},{2,4},{4,6},{6,8},{8,10},{10,12},{12,14},{14,16},{16,18},{18... | collective-permute-start | bytes 49160 | tf_op jit(solution)/shard_map/ppermute | solution.py:29
  4.5 103.5 %collective-permute-start.1 = (bf16[2,2,2048]{2,1,0:T(2,128)(2,1)S(1)}, bf16[2,2,2048]{2,1,0:T(2,128)(2,1)S(1)}, u32[]{:S(2)}, u32[]{:S(2)}) collective-permute-start(bf16[2,2,2048]{2,1,0:T(2,128)(2,1)S(1)} %get-tuple-element.418), channel_id=1, source_target_pairs={{2,0},{4,2},{6,4},{8,6},{10,8},{12,10},{14,12},{16,14},{18,16},{20... | collective-permute-start | bytes 49160 | tf_op jit(solution)/shard_map/ppermute | solution.py:31
  23.3 84.0 %copy-start = (f32[16,2048]{1,0:T(8,128)S(1)}, f32[16,2048]{1,0:T(8,128)}, u32[]{:S(2)}) copy-start(f32[16,2048]{1,0:T(8,128)} %param.11) | copy-start | bytes 393220
  23.3 84.0 %copy-start.1 = (f32[1,16,2048]{2,1,0:T(8,128)S(1)}, f32[1,16,2048]{2,1,0:T(8,128)}, u32[]{:S(2)}) copy-start(f32[1,16,2048]{2,1,0:T(8,128)} %param.10) | copy-start | bytes 393220
  97.9 78.3 %all-to-all-start = ((f32[128,4,1,6]{3,1,2,0:T(4,128)}), f32[128,4,1,6]{3,1,2,0:T(4,128)S(1)}, u32[]{:S(2)}, u32[]{:S(2)}) async-start(f32[128,4,1,6]{3,1,2,0:T(4,128)} %constant_dynamic-update-slice_fusion), calls=%async_computation | async-start | bytes 524288 | tf_op jit(solution)/shard_map/all_to_all | solution.py:12
  176.2 30.8 %all-to-all-start.1 = ((bf16[128,2,128]{2,1,0:T(2,128)(2,1)}), bf16[128,2,128]{2,1,0:T(2,128)(2,1)S(1)}, u32[]{:S(2)}, u32[]{:S(2)}) async-start(bf16[128,2,128]{2,1,0:T(2,128)(2,1)} %reshape.696), calls=%async_computation.1 | async-start | bytes 131072 | tf_op jit(solution)/shard_map/all_to_all | solution.py:108
  417.7 11.7 %collective-permute-start.2 = (bf16[1,2,2048]{2,1,0:T(2,128)(2,1)S(1)}, bf16[1,2,2048]{2,1,0:T(2,128)(2,1)S(1)}, u32[]{:S(2)}, u32[]{:S(2)}) collective-permute-start(bf16[1,2,2048]{2,1,0:T(2,128)(2,1)S(1)} %get-tuple-element.419), channel_id=1, source_target_pairs={{0,2},{2,4},{4,6},{6,8},{8,10},{10,12},{12,14},{14,16},{16,18},{18... | collective-permute-start | bytes 24584 | tf_op jit(solution)/shard_map/ppermute | solution.py:29
  420.3 10.4 %collective-permute-start.3 = (bf16[1,2,2048]{2,1,0:T(2,128)(2,1)S(1)}, bf16[1,2,2048]{2,1,0:T(2,128)(2,1)S(1)}, u32[]{:S(2)}, u32[]{:S(2)}) collective-permute-start(bf16[1,2,2048]{2,1,0:T(2,128)(2,1)S(1)} %get-tuple-element.420), channel_id=1, source_target_pairs={{2,0},{4,2},{6,4},{8,6},{10,8},{12,10},{14,12},{16,14},{18,16},{20... | collective-permute-start | bytes 24584 | tf_op jit(solution)/shard_map/ppermute | solution.py:31
